TPU v7x, 32 devices: a whole 2x2x4 slice. The times are simulated.
32 devices in a mesh: seq: 8 (over z, x), tp: 4 (over y, core).
Axes of the slice: x: 2, y: 2, z: 4, core: 2. Of those that a mesh axis runs over, the one named last changes fastest.
Arguments:
- hidden_in: bfloat16 [16, 2048], replicated, may hold values from -6 to 6
- lengths: int32 [16], replicated, may hold values from 1 to 511, 2431 in all
- positions: int32 [16], replicated, may hold values from 0 to 1023
- query_weight: bfloat16 [2, 2048, 2048], P(None, 'seq', 'tp'), may hold values from -0.125 to 0.125
- key_weight: bfloat16 [2, 2048, 512], P(None, 'seq', 'tp'), may hold values from -4 to 4
- value_weight: bfloat16 [2, 2048, 512], P(None, 'seq', 'tp'), may hold values from -0.125 to 0.125
- out_weight: bfloat16 [2, 2048, 2048], P(None, 'tp', 'seq'), may hold values from -0.125 to 0.125
- gate_weight: bfloat16 [2, 2048, 8192], P(None, 'seq', 'tp'), may hold values from -0.125 to 0.125
- up_weight: bfloat16 [2, 2048, 8192], P(None, 'seq', 'tp'), may hold values from -0.125 to 0.125
- down_weight: bfloat16 [2, 8192, 2048], P(None, 'tp', 'seq'), may hold values from -0.0625 to 0.0625
- key_cache: bfloat16 [2, 16, 512, 512], P(None, None, 'seq', 'tp'), may hold values from -80 to 80
- value_cache: bfloat16 [2, 16, 512, 512], P(None, None, 'seq', 'tp'), may hold values from -6 to 6
Outputs:
- hidden_out: bfloat16 [16, 2048], replicated
- key_out: bfloat16 [2, 16, 512, 512], P(None, None, 'seq', 'tp')
- value_out: bfloat16 [2, 16, 512, 512], P(None, None, 'seq', 'tp')
Inputs may be any that keep to these rules, and one draw needn't show every extreme that they name: Request b has its cached rows at positions 0 .. lengths[b] - 1 and its new token goes to row lengths[b]; rows above are padding. The longest request has exactly 511 cached rows.
All inputs are finite; a program needn't handle non-finite values.
Results may differ from a plain program's by a relative error of at most 0.015.
Values may be sent and summed in bfloat16 or wider, within the bound.
No kernel may reach another device: no remote copies, remote signals or barrier semaphores. Data moves between devices by JAX's collectives and lax.ppermute only.
A program may use at most 64 MiB of HBM per device.

v0:
```python
import math
import jax
import jax.numpy as jnp
from jax import lax
from jax.sharding import PartitionSpec as P

HEAD_DIM = 64
LAYERS = 2
eps_norm = 1e-05
neg_fill = -1e30


def rms_norm(stream):
    as_float = stream.astype(jnp.float32)
    spread = jnp.mean(as_float * as_float, axis=-1, keepdims=True)
    return (as_float * lax.rsqrt(spread + eps_norm)).astype(jnp.bfloat16)


def rotate(heads, positions):
    half_dim = heads.shape[-1] // 2
    inverse = 500000.0 ** (-(2.0 * jnp.arange(half_dim, dtype=jnp.float32)) / heads.shape[-1])
    angles = positions.astype(jnp.float32)[:, None] * inverse[None, :]
    cosine = jnp.cos(angles)[:, None, :]
    sine = jnp.sin(angles)[:, None, :]
    first_half = heads[..., :half_dim]
    second_half = heads[..., half_dim:]
    return jnp.concatenate(
        [first_half * cosine - second_half * sine, second_half * cosine + first_half * sine],
        axis=-1,
    )


def per_device(
    hidden_in,
    lengths,
    positions,
    query_weight,
    key_weight,
    value_weight,
    out_weight,
    gate_weight,
    up_weight,
    down_weight,
    key_cache,
    value_cache,
):
    seq_index = lax.axis_index("seq")
    row_count = query_weight.shape[1]
    row_start = seq_index * row_count
    col_count = out_weight.shape[2]
    col_start = seq_index * col_count
    block_len = key_cache.shape[2]
    kv_width_here = key_cache.shape[3]
    query_width = query_weight.shape[2]
    requests = hidden_in.shape[0]
    group_heads = query_width // HEAD_DIM
    kv_here = kv_width_here // HEAD_DIM
    repeat = group_heads // kv_here
    score_scale = 1.0 / math.sqrt(HEAD_DIM)
    global_slots = seq_index * block_len + jnp.arange(block_len, dtype=jnp.int32)
    new_slot = (global_slots[None, :] == lengths[:, None])[:, :, None]
    live_mask = (global_slots[None, :] <= lengths[:, None])[:, None, None, :]

    def finish(part_terms, stream_now):
        summed = lax.psum(part_terms, "tp")
        own_cols = lax.dynamic_slice_in_dim(stream_now, col_start, col_count, 1).astype(jnp.float32)
        return lax.all_gather((own_cols + summed).astype(jnp.bfloat16), "seq", axis=1, tiled=True)

    stream = hidden_in
    key_layers = []
    value_layers = []
    for layer_idx in range(LAYERS):
        normed = rms_norm(stream)
        own_rows = lax.dynamic_slice_in_dim(normed, row_start, row_count, 1)
        query_part = jnp.dot(own_rows, query_weight[layer_idx], preferred_element_type=jnp.float32)
        key_part = jnp.dot(own_rows, key_weight[layer_idx], preferred_element_type=jnp.float32)
        value_part = jnp.dot(own_rows, value_weight[layer_idx], preferred_element_type=jnp.float32)
        query, key_new, value_new = lax.psum((query_part, key_part, value_part), "seq")
        query = rotate(query.reshape(requests, group_heads, HEAD_DIM), positions).astype(
            jnp.bfloat16
        )
        query = query.reshape(requests, kv_here, repeat, HEAD_DIM)
        key_new = (
            rotate(key_new.reshape(requests, kv_here, HEAD_DIM), positions)
            .astype(jnp.bfloat16)
            .reshape(requests, kv_width_here)
        )
        value_new = value_new.astype(jnp.bfloat16)
        key_rows = jnp.where(new_slot, key_new[:, None, :], key_cache[layer_idx])
        value_rows = jnp.where(new_slot, value_new[:, None, :], value_cache[layer_idx])
        key_heads = key_rows.reshape(requests, block_len, kv_here, HEAD_DIM)
        value_heads = value_rows.reshape(requests, block_len, kv_here, HEAD_DIM)
        scores = (
            jnp.einsum("bkrd,bskd->bkrs", query, key_heads, preferred_element_type=jnp.float32)
            * score_scale
        )
        scores = jnp.where(live_mask, scores, neg_fill)
        row_top = lax.pmax(jnp.max(scores, axis=3), "seq")
        weights = jnp.where(live_mask, jnp.exp(scores - row_top[..., None]), 0.0)
        local_sums = jnp.sum(weights, axis=3)
        local_acc = jnp.einsum(
            "bkrs,bskd->bkrd",
            weights.astype(jnp.bfloat16),
            value_heads,
            preferred_element_type=jnp.float32,
        )
        totals, weighted = lax.psum((local_sums, local_acc), "seq")
        attended = (
            (weighted / totals[..., None]).astype(jnp.bfloat16).reshape(requests, query_width)
        )
        attn_terms = jnp.dot(attended, out_weight[layer_idx], preferred_element_type=jnp.float32)
        mid = finish(attn_terms, stream)
        normed_two = rms_norm(mid)
        rows_two = lax.dynamic_slice_in_dim(normed_two, row_start, row_count, 1)
        gate_part = jnp.dot(rows_two, gate_weight[layer_idx], preferred_element_type=jnp.float32)
        up_part = jnp.dot(rows_two, up_weight[layer_idx], preferred_element_type=jnp.float32)
        gate_sum, up_sum = lax.psum((gate_part, up_part), "seq")
        hidden = (jax.nn.silu(gate_sum) * up_sum).astype(jnp.bfloat16)
        down_terms = jnp.dot(hidden, down_weight[layer_idx], preferred_element_type=jnp.float32)
        stream = finish(down_terms, mid)
        key_layers.append(key_rows)
        value_layers.append(value_rows)
    return (stream, jnp.stack(key_layers), jnp.stack(value_layers))


def solution(mesh):
    return jax.shard_map(
        per_device,
        mesh=mesh,
        in_specs=(
            P(),
            P(),
            P(),
            P(None, "seq", "tp"),
            P(None, "seq", "tp"),
            P(None, "seq", "tp"),
            P(None, "tp", "seq"),
            P(None, "seq", "tp"),
            P(None, "seq", "tp"),
            P(None, "tp", "seq"),
            P(None, None, "seq", "tp"),
            P(None, None, "seq", "tp"),
        ),
        out_specs=(P(), P(None, None, "seq", "tp"), P(None, None, "seq", "tp")),
        check_vma=False,
    )
```

profile of v0, /device:TPU:0, one launch (start us, length us, event | category | flops | bytes accessed | tf_op | source)
XLA Modules:
  0.0 562.6 jit_solution(6855281874656980006)
XLA Ops:
  13.7 39.8 %all-reduce.3 = (bf16[16,128]{1,0:T(8,128)(2,1)S(1)}, f32[16,2,64]{2,1,0:T(2,128)S(1)}, f32[16,8,64]{2,1,0:T(8,128)S(1)}) all-reduce(f32[16,128]{1,0:T(8,128)S(1)} %fusion.46, f32[16,2,64]{2,1,0:T(2,128)S(1)} %reshape.206, f32[16,8,64]{2,1,0:T(8,128)S(1)} %reshape.205), channel_id=1, replica_groups=mesh['seq'=8,'tp'=4] {'seq'}, use_global_device_ids=true, to_apply=%region_5.6 | all-reduce | flops 12288 | bytes 94208 | tf_op jit(solution)/shard_map/psum | solution.py:78
  55.8 1.7 fusion.88
  57.5 33.0 %pmax.14 = f32[16,2,4]{2,1,0:T(2,128)S(1)} all-reduce(f32[16,2,4]{2,1,0:T(2,128)S(1)} %get-tuple-element.38), channel_id=1, replica_groups=mesh['seq'=8,'tp'=4] {'seq'}, use_global_device_ids=true, to_apply=%region_4.5 | all-reduce | flops 128 | bytes 1024 | tf_op jit(solution)/shard_map/pmax | solution.py:98
  91.8 33.8 %all-reduce.2 = (f32[16,2,4,64]{3,2,1,0:T(4,128)S(1)}, f32[16,2,4]{2,1,0:T(2,128)S(1)}) all-reduce(f32[16,2,4,64]{3,2,1,0:T(4,128)S(1)} %fusion.21, f32[16,2,4]{2,1,0:T(2,128)S(1)} %fusion.56), channel_id=1, replica_groups=mesh['seq'=8,'tp'=4] {'seq'}, use_global_device_ids=true, to_apply=%region_6.7 | all-reduce | flops 8320 | bytes 66560 | tf_op jit(solution)/shard_map/psum | solution.py:107
  126.0 10.1 %psum.131 = f32[16,256]{1,0:T(8,128)S(1)} all-reduce(f32[16,256]{1,0:T(8,128)S(1)} %fusion.30), channel_id=1, replica_groups=mesh['seq'=8,'tp'=4] {'tp'}, use_global_device_ids=true, to_apply=%region_9.10 | all-reduce | flops 4096 | bytes 32768 | tf_op jit(solution)/shard_map/psum | solution.py:65
  136.8 30.5 %all_gather.12 = bf16[16,2048]{1,0:T(8,128)(2,1)S(1)} all-gather(bf16[16,256]{1,0:T(8,128)(2,1)S(1)} %add_convert_fusion.5), channel_id=1, replica_groups=mesh['seq'=8,'tp'=4] {'seq'}, dimensions={1}, use_global_device_ids=true | all-gather | bytes 73728 | tf_op jit(solution)/shard_map/all_gather | solution.py:67
  168.4 2.3 fusion.12
  171.4 69.2 %all-reduce.11.cloned.1.call-done = (f32[16,2048]{1,0:T(8,128)}, f32[16,2048]{1,0:T(8,128)}) async-done(((f32[16,2048]{1,0:T(8,128)}, f32[16,2048]{1,0:T(8,128)}), (f32[16,2048]{1,0:T(8,128)}, f32[16,2048]{1,0:T(8,128)})) %all-reduce.11.cloned.1.call-update) | async-done | bytes 262160 | tf_op jit(solution)/shard_map/psum | solution.py:117
  240.6 1.6 fusion.8
  242.2 10.1 %psum.134 = f32[16,256]{1,0:T(8,128)S(1)} all-reduce(f32[16,256]{1,0:T(8,128)S(1)} %fusion.8), channel_id=1, replica_groups=mesh['seq'=8,'tp'=4] {'tp'}, use_global_device_ids=true, to_apply=%region_13.14 | all-reduce | flops 4096 | bytes 32768 | tf_op jit(solution)/shard_map/psum | solution.py:65
  252.3 30.5 %all_gather.13 = bf16[16,2048]{1,0:T(8,128)(2,1)S(1)} all-gather(bf16[16,256]{1,0:T(8,128)(2,1)S(1)} %add_convert_fusion.4), channel_id=1, replica_groups=mesh['seq'=8,'tp'=4] {'seq'}, dimensions={1}, use_global_device_ids=true | all-gather | bytes 73728 | tf_op jit(solution)/shard_map/all_gather | solution.py:67
  286.4 36.4 %all-reduce.1 = (bf16[16,128]{1,0:T(8,128)(2,1)S(1)}, f32[16,2,64]{2,1,0:T(2,128)S(1)}, f32[16,8,64]{2,1,0:T(8,128)S(1)}) all-reduce(f32[16,128]{1,0:T(8,128)S(1)} %fusion.42, f32[16,2,64]{2,1,0:T(2,128)S(1)} %reshape.209, f32[16,8,64]{2,1,0:T(8,128)S(1)} %reshape.208), channel_id=1, replica_groups=mesh['seq'=8,'tp'=4] {'seq'}, use_global_device_ids=true, to_apply=%region_19.20 | all-reduce | flops 12288 | bytes 94208 | tf_op jit(solution)/shard_map/psum | solution.py:78
  324.4 1.9 broadcast_select_fusion.1
  326.2 1.2 squeeze.67
  327.8 1.2 fusion.89
  329.0 33.0 %pmax.15 = f32[16,2,4]{2,1,0:T(2,128)S(1)} all-reduce(f32[16,2,4]{2,1,0:T(2,128)S(1)} %get-tuple-element.40), channel_id=1, replica_groups=mesh['seq'=8,'tp'=4] {'seq'}, use_global_device_ids=true, to_apply=%region_18.19 | all-reduce | flops 128 | bytes 1024 | tf_op jit(solution)/shard_map/pmax | solution.py:98
  364.0 34.0 %all-reduce = (f32[16,2,4,64]{3,2,1,0:T(4,128)S(1)}, f32[16,2,4]{2,1,0:T(2,128)S(1)}) all-reduce(f32[16,2,4,64]{3,2,1,0:T(4,128)S(1)} %fusion.20, f32[16,2,4]{2,1,0:T(2,128)S(1)} %fusion.58), channel_id=1, replica_groups=mesh['seq'=8,'tp'=4] {'seq'}, use_global_device_ids=true, to_apply=%region_20.21 | all-reduce | flops 8320 | bytes 66560 | tf_op jit(solution)/shard_map/psum | solution.py:107
  399.3 10.1 %psum.140 = f32[16,256]{1,0:T(8,128)S(1)} all-reduce(f32[16,256]{1,0:T(8,128)S(1)} %fusion.26), channel_id=1, replica_groups=mesh['seq'=8,'tp'=4] {'tp'}, use_global_device_ids=true, to_apply=%region_23.24 | all-reduce | flops 4096 | bytes 32768 | tf_op jit(solution)/shard_map/psum | solution.py:65
  409.4 30.5 %all_gather.14 = bf16[16,2048]{1,0:T(8,128)(2,1)S(1)} all-gather(bf16[16,256]{1,0:T(8,128)(2,1)S(1)} %add_convert_fusion.3), channel_id=1, replica_groups=mesh['seq'=8,'tp'=4] {'seq'}, dimensions={1}, use_global_device_ids=true | all-gather | bytes 73728 | tf_op jit(solution)/shard_map/all_gather | solution.py:67
  441.0 2.3 fusion.6
  444.4 68.8 %all-reduce.9.cloned.1.call-done = (f32[16,2048]{1,0:T(8,128)}, f32[16,2048]{1,0:T(8,128)}) async-done(((f32[16,2048]{1,0:T(8,128)}, f32[16,2048]{1,0:T(8,128)}), (f32[16,2048]{1,0:T(8,128)}, f32[16,2048]{1,0:T(8,128)})) %all-reduce.9.cloned.1.call-update) | async-done | bytes 262160 | tf_op jit(solution)/shard_map/psum | solution.py:117
  513.3 1.2 fusion.2
  514.5 10.1 %psum.143 = f32[16,256]{1,0:T(8,128)S(1)} all-reduce(f32[16,256]{1,0:T(8,128)S(1)} %fusion.2), channel_id=1, replica_groups=mesh['seq'=8,'tp'=4] {'tp'}, use_global_device_ids=true, to_apply=%region_27.28 | all-reduce | flops 4096 | bytes 32768 | tf_op jit(solution)/shard_map/psum | solution.py:65
  524.6 30.5 %all_gather.15 = bf16[16,2048]{1,0:T(8,128)(2,1)S(1)} all-gather(bf16[16,256]{1,0:T(8,128)(2,1)S(1)} %add_convert_fusion.2), channel_id=1, replica_groups=mesh['seq'=8,'tp'=4] {'seq'}, dimensions={1}, use_global_device_ids=true | all-gather | bytes 73728 | tf_op jit(solution)/shard_map/all_gather | solution.py:67
  (97 shorter events, 24.3 us)
Async XLA Ops:
  7.2 47.1 %slice-start = ((bf16[2,16,64,128]{3,2,1,0:T(8,128)(2,1)}), bf16[1,16,64,128]{3,2,1,0:T(8,128)(2,1)S(1)}, s32[]{:S(2)}) async-start(bf16[2,16,64,128]{3,2,1,0:T(8,128)(2,1)} %param.22), calls=%async_computation.2 | async-start | bytes 524288 | tf_op jit(solution)/shard_map/slice | solution.py:89
  7.2 48.1 %copy-start.15 = (s32[16]{0:T(128)S(1)}, s32[16]{0:T(128)}, u32[]{:S(2)}) copy-start(s32[16]{0:T(128)} %param.14) | copy-start | bytes 196
  7.2 48.5 %copy-start.13 = (s32[16]{0:T(128)S(1)}, s32[16]{0:T(128)}, u32[]{:S(2)}) copy-start(s32[16]{0:T(128)} %param.13) | copy-start | bytes 196
  7.2 233.4 %all-reduce.11.cloned.1.call-start = ((), (), s32[]{:S(2)}) async-start(), calls=%async_computation.1 | async-start | bytes 524288 | tf_op jit(solution)/shard_map/psum | solution.py:117
  53.6 0.7 copy-start.10
  54.3 71.6 %copy-start.7 = (bf16[2,512,256]{2,1,0:T(8,128)(2,1)S(1)}, bf16[2,512,256]{2,1,0:T(8,128)(2,1)}, u32[]{:S(2)}) copy-start(bf16[2,512,256]{2,1,0:T(8,128)(2,1)} %param.18) | copy-start | bytes 1572868
  55.5 111.9 %copy-start = (bf16[2,256,2048]{2,1,0:T(8,128)(2,1)S(1)}, bf16[2,256,2048]{2,1,0:T(8,128)(2,1)}, u32[]{:S(2)}) copy-start(bf16[2,256,2048]{2,1,0:T(8,128)(2,1)} %param.20) | copy-start | bytes 6291460
  55.7 112.7 %copy-start.9 = (pred[16,64]{1,0:T(8,128)(4,1)}, pred[16,64]{1,0:T(8,128)(4,1)S(1)}, u32[]{:S(2)}) copy-start(pred[16,64]{1,0:T(8,128)(4,1)S(1)} %get-tuple-element.34) | copy-start | bytes 3076
  55.7 112.7 %copy-start.12 = (pred[16,64]{1,0:T(8,128)(4,1)}, pred[16,64]{1,0:T(8,128)(4,1)S(1)}, u32[]{:S(2)}) copy-start(pred[16,64]{1,0:T(8,128)(4,1)S(1)} %get-tuple-element.35) | copy-start | bytes 3076
  168.4 155.9 %copy-start.1 = (bf16[2,16,64,128]{3,2,1,0:T(8,128)(2,1)S(1)}, bf16[2,16,64,128]{3,2,1,0:T(8,128)(2,1)}, u32[]{:S(2)}) copy-start(bf16[2,16,64,128]{3,2,1,0:T(8,128)(2,1)} %param.23) | copy-start | bytes 1572868
  168.4 155.9 %copy-start.2 = (bf16[2,16,64,128]{3,2,1,0:T(8,128)(2,1)S(1)}, bf16[2,16,64,128]{3,2,1,0:T(8,128)(2,1)}, u32[]{:S(2)}) copy-start(bf16[2,16,64,128]{3,2,1,0:T(8,128)(2,1)} %param.22) | copy-start | bytes 1572868
  170.7 342.6 %all-reduce.9.cloned.1.call-start = ((), (), s32[]{:S(2)}) async-start(), calls=%async_computation | async-start | bytes 524288 | tf_op jit(solution)/shard_map/psum | solution.py:117
  322.8 0.9 copy-start.11
  323.0 0.7 copy-start.8
  364.0 79.4 %copy-start.3 = (bf16[1,16,64,128]{3,2,1,0:T(8,128)(2,1)S(1)}, bf16[1,16,64,128]{3,2,1,0:T(8,128)(2,1)}, u32[]{:S(2)}) copy-start(bf16[1,16,64,128]{3,2,1,0:T(8,128)(2,1)} %get-tuple-element.17) | copy-start | bytes 786436
  364.0 79.4 %copy-start.4 = (bf16[1,16,64,128]{3,2,1,0:T(8,128)(2,1)S(1)}, bf16[1,16,64,128]{3,2,1,0:T(8,128)(2,1)}, u32[]{:S(2)}) copy-start(bf16[1,16,64,128]{3,2,1,0:T(8,128)(2,1)} %get-tuple-element.18) | copy-start | bytes 786436
  364.0 79.4 %copy-start.5 = (bf16[1,16,64,128]{3,2,1,0:T(8,128)(2,1)S(1)}, bf16[1,16,64,128]{3,2,1,0:T(8,128)(2,1)}, u32[]{:S(2)}) copy-start(bf16[1,16,64,128]{3,2,1,0:T(8,128)(2,1)} %get-tuple-element.32) | copy-start | bytes 786436
  364.0 79.4 %copy-start.6 = (bf16[1,16,64,128]{3,2,1,0:T(8,128)(2,1)S(1)}, bf16[1,16,64,128]{3,2,1,0:T(8,128)(2,1)}, u32[]{:S(2)}) copy-start(bf16[1,16,64,128]{3,2,1,0:T(8,128)(2,1)} %get-tuple-element.33) | copy-start | bytes 786436
  441.0 72.3 %copy-start.14 = (bf16[2,2048,256]{2,1,0:T(8,128)(2,1)S(1)}, bf16[2,2048,256]{2,1,0:T(8,128)(2,1)}, u32[]{:S(2)}) copy-start(bf16[2,2048,256]{2,1,0:T(8,128)(2,1)} %param.21) | copy-start | bytes 6291460
Sparse Core Ops, SparseCore 0:
  170.8 69.7 all-reduce.10
  443.5 69.7 all-reduce.8
where the time goes:
time: 564 us; the launch traced here: 563 us
  blocking collectives  372 us (66%)
  waiting for transfers between devices  138 us (24%)
  matrix products  22 us (4%)
  between operations  14.4 us (3%)
  other arithmetic  8.02 us (1%)
  local copies, waits for them, and re-layouts  7.62 us (1%)
    psum x2, waiting for transfers between devices, per_device(): gate_sum, up_sum = lax.psum((gate_part, up_part), 'seq')  138 us
    all_gather x4, blocking collectives, finish(): lax.all_gather((own_cols + summed).astype(jnp.bfloat16), 'seq', axis=1, t...  122 us
    psum x2, blocking collectives, per_device(): lax.psum((query_part, key_part, value_part), 'seq')  76.3 us
    psum x2, blocking collectives, per_device(): totals, weighted = lax.psum((local_sums, local_acc), 'seq')  67.8 us
    pmax x2, blocking collectives, per_device(): row_top = lax.pmax(jnp.max(scores, axis=3), 'seq')  66 us
    psum x4, blocking collectives, finish(): summed = lax.psum(part_terms, 'tp')  40.5 us
  transfers between devices with their start and end apart: 2, of which 2 were waited for; matrix products, arithmetic and copies ran while one was open for 0% of the time, Pallas kernels for 0%

commit v1 on v0

--- a/solution.py
+++ b/solution.py
@@ -64,7 +64,20 @@
     def finish(part_terms, stream_now):
         summed = lax.psum(part_terms, "tp")
         own_cols = lax.dynamic_slice_in_dim(stream_now, col_start, col_count, 1).astype(jnp.float32)
-        return lax.all_gather((own_cols + summed).astype(jnp.bfloat16), "seq", axis=1, tiled=True)
+
+        def perform_the_sheet(patch):
+            step_out = lax.axis_size("seq")
+            y, extra = (step_out, lax.axis_index("seq"))
+            mixed_arr, b_next = (patch, 1)
+            while b_next < y:
+                r1 = lax.ppermute(mixed_arr, "seq", [(num, num ^ b_next) for num in range(y)])
+                lower = jnp.concatenate([mixed_arr, r1], 1)
+                piece_next = jnp.concatenate([r1, mixed_arr], 1)
+                mixed_arr = jnp.where(extra & b_next == 0, lower, piece_next)
+                b_next = 2 * b_next
+            return mixed_arr
+
+        return perform_the_sheet((own_cols + summed).astype(jnp.bfloat16))
 
     stream = hidden_in
     key_layers = []

time: 564 us -> 492 us (0.87)
  blocking collectives: 372 us -> 250 us
  waiting for transfers between devices: 138 us -> 180 us
  starting transfers between devices: 0.08 us -> 7.82 us
    all_gather x4 -> x0, blocking collectives: 122 us -> none  [finish(): lax.all_gather((own_cols + summed).astype(jnp.bfloat16), 'seq', axis=1, t...]
    ppermute x0 -> x12, waiting for transfers between devices: none -> 39.7 us  [perform_the_sheet(): lax.ppermute(mixed_arr, 'seq', [(num, num ^ b_next) for num in range(y)])]
    ppermute x0 -> x12, starting transfers between devices: none -> 7.74 us  [perform_the_sheet(): lax.ppermute(mixed_arr, 'seq', [(num, num ^ b_next) for num in range(y)])]
  transfers between devices with their start and end apart: 2 -> 14, of which waited for: 2 -> 14; matrix products, arithmetic and copies ran while one was open for 0% -> 0% of each run, Pallas kernels for 0% -> 0%
where the time goes in v1:
time: 492 us; the launch traced here: 491 us
  blocking collectives  250 us (51%)
  waiting for transfers between devices  180 us (37%)
  matrix products  21.6 us (4%)
  between operations  14.5 us (3%)
  other arithmetic  8.73 us (2%)
  starting transfers between devices  7.82 us (2%)
  local copies, waits for them, and re-layouts  7.79 us (2%)
    psum x2, waiting for transfers between devices, per_device(): gate_sum, up_sum = lax.psum((gate_part, up_part), 'seq')  140 us
    psum x2, blocking collectives, per_device(): lax.psum((query_part, key_part, value_part), 'seq')  76.3 us
    psum x2, blocking collectives, per_device(): totals, weighted = lax.psum((local_sums, local_acc), 'seq')  67.7 us
    pmax x2, blocking collectives, per_device(): row_top = lax.pmax(jnp.max(scores, axis=3), 'seq')  66 us
    psum x4, blocking collectives, finish(): summed = lax.psum(part_terms, 'tp')  40.5 us
    ppermute x12, waiting for transfers between devices, perform_the_sheet(): lax.ppermute(mixed_arr, 'seq', [(num, num ^ b_next) for num in range(y)])  39.7 us
  transfers between devices with their start and end apart: 14, of which 14 were waited for; matrix products, arithmetic and copies ran while one was open for 0% of the time, Pallas kernels for 0%

profile of v1, /device:TPU:0, one launch (start us, length us, event | category | flops | bytes accessed | tf_op | source)
XLA Modules:
  0.0 490.6 jit_solution(9308082766792576374)
XLA Ops:
  13.7 39.8 %all-reduce.3 = (bf16[16,128]{1,0:T(8,128)(2,1)S(1)}, f32[16,2,64]{2,1,0:T(2,128)S(1)}, f32[16,8,64]{2,1,0:T(8,128)S(1)}) all-reduce(f32[16,128]{1,0:T(8,128)S(1)} %fusion.46, f32[16,2,64]{2,1,0:T(2,128)S(1)} %reshape.206, f32[16,8,64]{2,1,0:T(8,128)S(1)} %reshape.205), channel_id=1, replica_groups=mesh['seq'=8,'tp'=4] {'seq'}, use_global_device_ids=true, to_apply=%region_5.6 | all-reduce | flops 12288 | bytes 94208 | tf_op jit(solution)/shard_map/psum | solution.py:91
  57.5 33.0 %pmax.14 = f32[16,2,4]{2,1,0:T(2,128)S(1)} all-reduce(f32[16,2,4]{2,1,0:T(2,128)S(1)} %get-tuple-element.44), channel_id=1, replica_groups=mesh['seq'=8,'tp'=4] {'seq'}, use_global_device_ids=true, to_apply=%region_4.5 | all-reduce | flops 128 | bytes 1024 | tf_op jit(solution)/shard_map/pmax | solution.py:111
  91.8 33.8 %all-reduce.2 = (f32[16,2,4,64]{3,2,1,0:T(4,128)S(1)}, f32[16,2,4]{2,1,0:T(2,128)S(1)}) all-reduce(f32[16,2,4,64]{3,2,1,0:T(4,128)S(1)} %fusion.21, f32[16,2,4]{2,1,0:T(2,128)S(1)} %fusion.56), channel_id=1, replica_groups=mesh['seq'=8,'tp'=4] {'seq'}, use_global_device_ids=true, to_apply=%region_6.7 | all-reduce | flops 8320 | bytes 66560 | tf_op jit(solution)/shard_map/psum | solution.py:120
  126.0 10.1 %psum.131 = f32[16,256]{1,0:T(8,128)S(1)} all-reduce(f32[16,256]{1,0:T(8,128)S(1)} %fusion.30), channel_id=1, replica_groups=mesh['seq'=8,'tp'=4] {'tp'}, use_global_device_ids=true, to_apply=%region_9.10 | all-reduce | flops 4096 | bytes 32768 | tf_op jit(solution)/shard_map/psum | solution.py:65
  136.8 3.6 collective-permute-done
  140.5 3.7 collective-permute-done.1
  144.3 4.8 collective-permute-done.2
  150.2 2.3 fusion.12
  152.6 70.0 %all-reduce.11.cloned.1.call-done = (f32[16,2048]{1,0:T(8,128)}, f32[16,2048]{1,0:T(8,128)}) async-done(((f32[16,2048]{1,0:T(8,128)}, f32[16,2048]{1,0:T(8,128)}), (f32[16,2048]{1,0:T(8,128)}, f32[16,2048]{1,0:T(8,128)})) %all-reduce.11.cloned.1.call-update) | async-done | bytes 262160 | tf_op jit(solution)/shard_map/psum | solution.py:130
  224.2 10.1 %psum.134 = f32[16,256]{1,0:T(8,128)S(1)} all-reduce(f32[16,256]{1,0:T(8,128)S(1)} %fusion.8), channel_id=1, replica_groups=mesh['seq'=8,'tp'=4] {'tp'}, use_global_device_ids=true, to_apply=%region_13.14 | all-reduce | flops 4096 | bytes 32768 | tf_op jit(solution)/shard_map/psum | solution.py:65
  235.1 2.9 collective-permute-done.3
  239.0 2.7 collective-permute-done.4
  244.3 2.3 collective-permute-done.5
  250.2 36.4 %all-reduce.1 = (bf16[16,128]{1,0:T(8,128)(2,1)S(1)}, f32[16,2,64]{2,1,0:T(2,128)S(1)}, f32[16,8,64]{2,1,0:T(8,128)S(1)}) all-reduce(f32[16,128]{1,0:T(8,128)S(1)} %fusion.42, f32[16,2,64]{2,1,0:T(2,128)S(1)} %reshape.209, f32[16,8,64]{2,1,0:T(8,128)S(1)} %reshape.208), channel_id=1, replica_groups=mesh['seq'=8,'tp'=4] {'seq'}, use_global_device_ids=true, to_apply=%region_19.20 | all-reduce | flops 12288 | bytes 94208 | tf_op jit(solution)/shard_map/psum | solution.py:91
  294.0 33.0 %pmax.15 = f32[16,2,4]{2,1,0:T(2,128)S(1)} all-reduce(f32[16,2,4]{2,1,0:T(2,128)S(1)} %get-tuple-element.46), channel_id=1, replica_groups=mesh['seq'=8,'tp'=4] {'seq'}, use_global_device_ids=true, to_apply=%region_18.19 | all-reduce | flops 128 | bytes 1024 | tf_op jit(solution)/shard_map/pmax | solution.py:111
  328.9 33.9 %all-reduce = (f32[16,2,4,64]{3,2,1,0:T(4,128)S(1)}, f32[16,2,4]{2,1,0:T(2,128)S(1)}) all-reduce(f32[16,2,4,64]{3,2,1,0:T(4,128)S(1)} %fusion.20, f32[16,2,4]{2,1,0:T(2,128)S(1)} %fusion.58), channel_id=1, replica_groups=mesh['seq'=8,'tp'=4] {'seq'}, use_global_device_ids=true, to_apply=%region_20.21 | all-reduce | flops 8320 | bytes 66560 | tf_op jit(solution)/shard_map/psum | solution.py:120
  363.2 10.1 %psum.140 = f32[16,256]{1,0:T(8,128)S(1)} all-reduce(f32[16,256]{1,0:T(8,128)S(1)} %fusion.26), channel_id=1, replica_groups=mesh['seq'=8,'tp'=4] {'tp'}, use_global_device_ids=true, to_apply=%region_23.24 | all-reduce | flops 4096 | bytes 32768 | tf_op jit(solution)/shard_map/psum | solution.py:65
  373.4 3.6 collective-permute-done.6
  377.0 3.7 collective-permute-done.7
  380.9 4.8 collective-permute-done.8
  389.0 70.1 %all-reduce.9.cloned.1.call-done = (f32[16,2048]{1,0:T(8,128)}, f32[16,2048]{1,0:T(8,128)}) async-done(((f32[16,2048]{1,0:T(8,128)}, f32[16,2048]{1,0:T(8,128)}), (f32[16,2048]{1,0:T(8,128)}, f32[16,2048]{1,0:T(8,128)})) %all-reduce.9.cloned.1.call-update) | async-done | bytes 262160 | tf_op jit(solution)/shard_map/psum | solution.py:130
  460.7 10.1 %psum.143 = f32[16,256]{1,0:T(8,128)S(1)} all-reduce(f32[16,256]{1,0:T(8,128)S(1)} %fusion.2), channel_id=1, replica_groups=mesh['seq'=8,'tp'=4] {'tp'}, use_global_device_ids=true, to_apply=%region_27.28 | all-reduce | flops 4096 | bytes 32768 | tf_op jit(solution)/shard_map/psum | solution.py:65
  471.6 2.9 collective-permute-done.9
  475.5 2.7 collective-permute-done.10
  (125 shorter events, 45.7 us)
Async XLA Ops:
  7.2 215.4 %all-reduce.11.cloned.1.call-start = ((), (), s32[]{:S(2)}) async-start(), calls=%async_computation.1 | async-start | bytes 524288 | tf_op jit(solution)/shard_map/psum | solution.py:130
  55.5 93.7 %copy-start = (bf16[2,256,2048]{2,1,0:T(8,128)(2,1)S(1)}, bf16[2,256,2048]{2,1,0:T(8,128)(2,1)}, u32[]{:S(2)}) copy-start(bf16[2,256,2048]{2,1,0:T(8,128)(2,1)} %param.20) | copy-start | bytes 6291460
  55.7 94.5 %copy-start.10 = (pred[16,64]{1,0:T(8,128)(4,1)}, pred[16,64]{1,0:T(8,128)(4,1)S(1)}, u32[]{:S(2)}) copy-start(pred[16,64]{1,0:T(8,128)(4,1)S(1)} %get-tuple-element.40) | copy-start | bytes 3076
  55.7 94.5 %copy-start.13 = (pred[16,64]{1,0:T(8,128)(4,1)}, pred[16,64]{1,0:T(8,128)(4,1)S(1)}, u32[]{:S(2)}) copy-start(pred[16,64]{1,0:T(8,128)(4,1)S(1)} %get-tuple-element.41) | copy-start | bytes 3076
  136.8 3.7 collective-permute-start
  140.5 3.7 collective-permute-start.1
  144.2 4.9 collective-permute-start.2
  150.2 137.9 %copy-start.1 = (bf16[2,16,64,128]{3,2,1,0:T(8,128)(2,1)S(1)}, bf16[2,16,64,128]{3,2,1,0:T(8,128)(2,1)}, u32[]{:S(2)}) copy-start(bf16[2,16,64,128]{3,2,1,0:T(8,128)(2,1)} %param.23) | copy-start | bytes 1572868
  150.2 137.9 %copy-start.2 = (bf16[2,16,64,128]{3,2,1,0:T(8,128)(2,1)S(1)}, bf16[2,16,64,128]{3,2,1,0:T(8,128)(2,1)}, u32[]{:S(2)}) copy-start(bf16[2,16,64,128]{3,2,1,0:T(8,128)(2,1)} %param.22) | copy-start | bytes 1572868
  152.5 306.5 %all-reduce.9.cloned.1.call-start = ((), (), s32[]{:S(2)}) async-start(), calls=%async_computation | async-start | bytes 524288 | tf_op jit(solution)/shard_map/psum | solution.py:130
  234.3 3.7 collective-permute-start.3
  238.0 3.7 collective-permute-start.4
  241.8 4.9 collective-permute-start.5
  291.3 71.8 %copy-start.8 = (bf16[2,512,256]{2,1,0:T(8,128)(2,1)S(1)}, bf16[2,512,256]{2,1,0:T(8,128)(2,1)}, u32[]{:S(2)}) copy-start(bf16[2,512,256]{2,1,0:T(8,128)(2,1)} %param.18) | copy-start | bytes 1572868
  373.3 3.7 collective-permute-start.6
  377.0 3.7 collective-permute-start.7
  380.8 4.9 collective-permute-start.8
  385.8 94.3 %copy-start.3 = (bf16[1,16,64,128]{3,2,1,0:T(8,128)(2,1)S(1)}, bf16[1,16,64,128]{3,2,1,0:T(8,128)(2,1)}, u32[]{:S(2)}) copy-start(bf16[1,16,64,128]{3,2,1,0:T(8,128)(2,1)} %get-tuple-element.23) | copy-start | bytes 786436
  385.8 94.3 %copy-start.4 = (bf16[1,16,64,128]{3,2,1,0:T(8,128)(2,1)S(1)}, bf16[1,16,64,128]{3,2,1,0:T(8,128)(2,1)}, u32[]{:S(2)}) copy-start(bf16[1,16,64,128]{3,2,1,0:T(8,128)(2,1)} %get-tuple-element.24) | copy-start | bytes 786436
  385.9 94.3 %copy-start.5 = (bf16[1,16,64,128]{3,2,1,0:T(8,128)(2,1)S(1)}, bf16[1,16,64,128]{3,2,1,0:T(8,128)(2,1)}, u32[]{:S(2)}) copy-start(bf16[1,16,64,128]{3,2,1,0:T(8,128)(2,1)} %get-tuple-element.38) | copy-start | bytes 786436
  385.9 94.3 %copy-start.6 = (bf16[1,16,64,128]{3,2,1,0:T(8,128)(2,1)S(1)}, bf16[1,16,64,128]{3,2,1,0:T(8,128)(2,1)}, u32[]{:S(2)}) copy-start(bf16[1,16,64,128]{3,2,1,0:T(8,128)(2,1)} %get-tuple-element.39) | copy-start | bytes 786436
  470.8 3.7 collective-permute-start.9
  474.5 3.7 collective-permute-start.10
  478.3 4.9 collective-permute-start.11
  (7 other events, 217.5 us)
Sparse Core Ops, SparseCore 0:
  152.7 69.8 all-reduce.10
  389.1 69.8 all-reduce.8
